TPU v7x, 256 devices: a whole 4x4x8 slice. The times are simulated.
256 devices in a mesh: lead: 16 (over z, core), grp: 16 (over x, y).
Axes of the slice: x: 4, y: 4, z: 8, core: 2. Of those that a mesh axis runs over, the one named last changes fastest.
Arguments:
- matrix_tiles: bfloat16 [512, 384, 384], P(('lead', 'grp')), may hold values from -0.0546875 to 0.0546875
- tile_slot: int32 [16, 32], P('lead'), may hold values from 0 to 31, each once within a row
- tile_cols: int32 [64, 8], P('lead'), may hold values from 0 to 7, as said below
- send_rows: int32 [16, 2, 2], replicated, may hold values from 0 to 3, as said below
- residual: float32 [24576, 128], P(('lead', 'grp')), may hold values from -6 to 6
- diag_inv: float32 [24576], P(('lead', 'grp')), may hold values from 0.25 to 1
Outputs:
- correction: float32 [24576, 128], P(('lead', 'grp'))
Inputs may be any that keep to these rules, and one draw needn't show every extreme that they name: `tile_cols`: entry 0 of every row is that row's own block row within its leader, r for row l * 4 + r; indices below 4 are the leader's own block rows, the next 2 are the rows received from leader l - 1, the last 2 those received from leader l + 1 (cyclic). `send_rows`: the 2 entries of each list are distinct block rows of the sending leader.
All inputs are finite; a program needn't handle non-finite values.
Results may differ from a plain program's by a relative error of at most 0.0013.
Values may be sent and summed in bfloat16 or wider, within the bound.
No kernel may reach another device: no remote copies, remote signals or barrier semaphores. Data moves between devices by JAX's collectives and lax.ppermute only.
A program may use at most 64 MiB of HBM per device.

v0:
```python
import jax
import jax.numpy as jnp
from jax import lax
from jax.sharding import PartitionSpec as P

TILES_ROW = 8
lower_bound = 0.5
upper_bound = 1.5


def from_behind(shard, axis, by):
    devices = lax.axis_size(axis)
    return lax.ppermute(shard, axis, [(i, (i + by) % devices) for i in range(devices)])


def one_sweep(start_residual, inverse, apply_operator):
    center_value = (upper_bound + lower_bound) / 2.0
    half_width = (upper_bound - lower_bound) / 2.0
    ratio_value = center_value / half_width
    update = inverse[:, None] * start_residual / center_value
    approx = update
    rho_now = 1.0 / ratio_value
    rho_next = 1.0 / (2.0 * ratio_value - rho_now)
    remaining = start_residual - apply_operator(approx)
    update = (
        rho_next * rho_now * update + 2.0 * rho_next / half_width * inverse[:, None] * remaining
    )
    approx = approx + update
    return approx


def smooth_twice(rhs_field, inverse, apply_operator):
    first_pass = one_sweep(rhs_field, inverse, apply_operator)
    remaining = rhs_field - apply_operator(first_pass)
    second_pass = one_sweep(remaining, inverse, apply_operator)
    return first_pass + second_pass


def extend(blocks, send_rows):
    position = lax.axis_index("lead")
    mine_up = jnp.take(blocks, send_rows[position, 0], axis=0)
    mine_down = jnp.take(blocks, send_rows[position, 1], axis=0)
    from_lower = from_behind(mine_up, "lead", 1)
    from_upper = from_behind(mine_down, "lead", -1)
    return jnp.concatenate([blocks, from_lower, from_upper], axis=0)


def local(matrix_tiles, tile_slot, tile_cols, send_rows, residual, diag_inv):
    block_rows = tile_cols.shape[0]
    tile_size = matrix_tiles.shape[1]
    member = lax.axis_index("grp")
    share_rows = residual.shape[0]
    group_slots = tile_slot[0]
    group_tiles = lax.all_gather(matrix_tiles, "grp", axis=0, tiled=True)
    full_residual, full_inverse = (
        lax.all_gather(residual, "grp", axis=0, tiled=True),
        lax.all_gather(diag_inv, "grp", axis=0, tiled=True),
    )
    placed = (
        jnp.zeros_like(group_slots)
        .at[group_slots]
        .set(jnp.arange(group_slots.shape[0], dtype=jnp.int32))
    )
    ordered = jnp.take(group_tiles, placed, axis=0)
    ordered = ordered.reshape(block_rows, TILES_ROW, tile_size, tile_size)
    flat_cols = tile_cols.reshape(-1)

    def apply_operator(approx):
        rounded = approx.astype(jnp.bfloat16).reshape(block_rows, tile_size, -1)
        extended = extend(rounded, send_rows)
        operand = jnp.take(extended, flat_cols, axis=0).reshape(
            block_rows, TILES_ROW, tile_size, -1
        )
        coupled = jnp.einsum("rkij,rkjn->rin", ordered, operand, preferred_element_type=jnp.float32)
        return approx / full_inverse[:, None] + coupled.reshape(block_rows * tile_size, -1)

    whole_result = smooth_twice(full_residual, full_inverse, apply_operator)
    correction = lax.dynamic_slice_in_dim(whole_result, member * share_rows, share_rows, 0)
    return correction


def solution(mesh):
    in_specs = (
        P(("lead", "grp"), None, None),
        P("lead", None),
        P("lead", None),
        P(),
        P(("lead", "grp"), None),
        P(("lead", "grp")),
    )
    out_specs = P(("lead", "grp"), None)
    return jax.shard_map(local, mesh=mesh, in_specs=in_specs, out_specs=out_specs, check_vma=False)
```

profile of v0, /device:TPU:97, one launch (start us, length us, event | category | flops | bytes accessed | tf_op | source)
XLA Modules:
  0.0 167.3 jit_solution(6383218233879301720)
XLA Ops:
  6.5 0.7 all-gather.2.cloned.1.call-update
  7.3 1.3 dynamic-slice
  9.2 0.9 dynamic-update-slice
  10.1 0.9 fusion.14
  11.0 34.7 %all-reduce = f32[1536]{0:T(1024)S(1)} all-reduce(f32[1536]{0:T(1024)S(1)} %dynamic-update-slice), channel_id=1, replica_groups=mesh['lead'=16,'grp'=16] {'grp'}, use_global_device_ids=true, to_apply=%add | all-reduce | flops 1536 | bytes 12288
  45.7 21.1 %all_gather.10 = f32[1536,128]{1,0:T(8,128)S(1)} all-gather(f32[96,128]{1,0:T(8,128)} %param.14), channel_id=1, replica_groups=mesh['lead'=16,'grp'=16] {'grp'}, dimensions={0}, use_global_device_ids=true | all-gather | bytes 835584 | tf_op jit(solution)/shard_map/all_gather | solution.py:56
  67.8 13.9 %collective-permute-start = (bf16[2,384,128]{2,1,0:T(8,128)(2,1)S(1)}, bf16[2,384,128]{2,1,0:T(8,128)(2,1)S(1)}, u32[]{:S(2)}, u32[]{:S(2)}) collective-permute-start(bf16[2,384,128]{2,1,0:T(8,128)(2,1)S(1)} %broadcast_select_fusion.12), channel_id=1, source_target_pairs={{0,16},{16,32},{32,48},{48,64},{64,80},{80,96},{96,112},{112,128},... | collective-permute-start | bytes 589832 | tf_op jit(solution)/shard_map/ppermute | solution.py:13
  82.6 0.7 scatter_custom_fusion
  83.5 0.9 collective-permute-done
  84.4 4.8 %collective-permute-done.1 = bf16[2,384,128]{2,1,0:T(8,128)(2,1)S(1)} collective-permute-done((bf16[2,384,128]{2,1,0:T(8,128)(2,1)S(1)}, bf16[2,384,128]{2,1,0:T(8,128)(2,1)S(1)}, u32[]{:S(2)}, u32[]{:S(2)}) %collective-permute-start.1) | collective-permute-done | bytes 196640 | tf_op jit(solution)/shard_map/ppermute | solution.py:13
  89.3 2.6 %gather_fusion.3 = bf16[32,384,128]{2,1,0:T(8,128)(2,1)} fusion(bf16[8,384,128]{2,1,0:T(8,128)(2,1)S(1)} %pad_maximum_fusion, s32[1024]{0:T(1024)S(1)} %pad_clamp_fusion), kind=kCustom, calls=%fused_computation.1.clone | custom fusion | bytes 6291584 | tf_op jit(solution)/shard_map/jit(_take)/gather | solution.py:71
  91.9 3.9 %broadcast_select_fusion.6 = bf16[32,384,128]{2,1,0:T(8,128)(2,1)} fusion(bf16[32,384,128]{2,1,0:T(8,128)(2,1)} %gather_fusion.3, pred[32]{0:T(512)(128)(4,1)S(1)} %compare_and_fusion), kind=kLoop, calls=%fused_computation.20 | loop fusion | flops 1572864 | bytes 6291488 | tf_op jit(solution)/shard_map/jit(_take)/select_n | solution.py:71
  96.0 9.8 %gather_fusion = bf16[32,384,384]{2,1,0:T(8,128)(2,1)} fusion(bf16[32,384,384]{2,1,0:T(8,128)(2,1)} %all-gather.2.cloned.1.call-done, s32[1024]{0:T(1024)S(1)} %pad_clamp_fusion.3), kind=kCustom, calls=%fused_computation.9 | custom fusion | bytes 18874496 | tf_op jit(solution)/shard_map/jit(_take)/gather | solution.py:64
  105.7 7.3 %fusion.2 = f32[4,384,128,1]{2,1,3,0:T(8,128)S(1)} fusion(bf16[4,8,384,128]{3,2,1,0:T(8,128)(2,1)} %bitcast.54, bf16[4,8,384,384]{3,2,1,0:T(8,128)(2,1)} %bitcast.42, pred[4,8]{1,0:T(4,128)(4,1)S(1)} %broadcast_in_dim.40), kind=kOutput, calls=%fused_computation.14 | convolution fusion | flops 1212678144 | bytes 13369376 | tf_op jit(solution)/shard_map/rkij,rkjn->rin/dot_general | solution.py:74
  114.9 3.2 %collective-permute-start.2 = (bf16[2,384,128]{2,1,0:T(8,128)(2,1)S(1)}, bf16[2,384,128]{2,1,0:T(8,128)(2,1)S(1)}, u32[]{:S(2)}, u32[]{:S(2)}) collective-permute-start(bf16[2,384,128]{2,1,0:T(8,128)(2,1)S(1)} %broadcast_select_fusion.11), channel_id=1, source_target_pairs={{0,16},{16,32},{32,48},{48,64},{64,80},{80,96},{96,112},{112,128},... | collective-permute-start | bytes 589832 | tf_op jit(solution)/shard_map/ppermute | solution.py:13
  118.2 2.6 %collective-permute-done.2 = bf16[2,384,128]{2,1,0:T(8,128)(2,1)S(1)} collective-permute-done((bf16[2,384,128]{2,1,0:T(8,128)(2,1)S(1)}, bf16[2,384,128]{2,1,0:T(8,128)(2,1)S(1)}, u32[]{:S(2)}, u32[]{:S(2)}) %collective-permute-start.2) | collective-permute-done | bytes 196640 | tf_op jit(solution)/shard_map/ppermute | solution.py:13
  120.8 3.7 %collective-permute-done.3 = bf16[2,384,128]{2,1,0:T(8,128)(2,1)S(1)} collective-permute-done((bf16[2,384,128]{2,1,0:T(8,128)(2,1)S(1)}, bf16[2,384,128]{2,1,0:T(8,128)(2,1)S(1)}, u32[]{:S(2)}, u32[]{:S(2)}) %collective-permute-start.3) | collective-permute-done | bytes 196640 | tf_op jit(solution)/shard_map/ppermute | solution.py:13
  124.6 2.6 %gather_fusion.6 = bf16[32,384,128]{2,1,0:T(8,128)(2,1)} fusion(bf16[8,384,128]{2,1,0:T(8,128)(2,1)S(1)} %pad_maximum_fusion.1, s32[1024]{0:T(1024)S(1)} %pad_clamp_fusion), kind=kCustom, calls=%fused_computation.7.clone | custom fusion | bytes 6291584 | tf_op jit(solution)/shard_map/jit(_take)/gather | solution.py:71
  127.2 2.3 %broadcast_select_fusion.5 = bf16[32,384,128]{2,1,0:T(8,128)(2,1)S(1)} fusion(bf16[32,384,128]{2,1,0:T(8,128)(2,1)} %gather_fusion.6, pred[32]{0:T(512)(128)(4,1)S(1)} %compare_and_fusion), kind=kLoop, calls=%fused_computation.19 | loop fusion | flops 1572864 | bytes 6291488 | tf_op jit(solution)/shard_map/jit(_take)/select_n | solution.py:71
  129.4 6.4 %fusion.1 = f32[4,384,128,1]{2,1,3,0:T(8,128)S(1)} fusion(bf16[4,8,384,128]{3,2,1,0:T(8,128)(2,1)S(1)} %bitcast.56, bf16[4,8,384,384]{3,2,1,0:T(8,128)(2,1)} %bitcast.43, pred[4,8]{1,0:T(4,128)(4,1)S(1)} %broadcast_in_dim.40), kind=kOutput, calls=%fused_computation.13 | convolution fusion | flops 1212678144 | bytes 13369376 | tf_op jit(solution)/shard_map/rkij,rkjn->rin/dot_general | solution.py:74
  135.8 1.3 broadcast_divide_fusion
  137.2 0.7 gather_fusion.8
  137.9 0.7 gather_fusion.7
  138.6 0.7 broadcast_select_fusion.7
  139.3 0.7 broadcast_select_fusion.10
  140.6 2.0 %collective-permute-done.4 = bf16[2,384,128]{2,1,0:T(8,128)(2,1)S(1)} collective-permute-done((bf16[2,384,128]{2,1,0:T(8,128)(2,1)S(1)}, bf16[2,384,128]{2,1,0:T(8,128)(2,1)S(1)}, u32[]{:S(2)}, u32[]{:S(2)}) %collective-permute-start.4) | collective-permute-done | bytes 196640 | tf_op jit(solution)/shard_map/ppermute | solution.py:13
  143.3 3.1 %collective-permute-done.5 = bf16[2,384,128]{2,1,0:T(8,128)(2,1)} collective-permute-done((bf16[2,384,128]{2,1,0:T(8,128)(2,1)S(1)}, bf16[2,384,128]{2,1,0:T(8,128)(2,1)}, u32[]{:S(2)}, u32[]{:S(2)}) %collective-permute-start.5) | collective-permute-done | bytes 196640 | tf_op jit(solution)/shard_map/ppermute | solution.py:13
  146.5 1.1 pad_maximum_fusion.2
  147.6 2.7 %gather_fusion.9 = bf16[32,384,128]{2,1,0:T(8,128)(2,1)} fusion(bf16[8,384,128]{2,1,0:T(8,128)(2,1)S(1)} %pad_maximum_fusion.2, s32[1024]{0:T(1024)} %copy-done.1), kind=kCustom, calls=%fused_computation.8.clone | custom fusion | bytes 6291584 | tf_op jit(solution)/shard_map/jit(_take)/gather | solution.py:71
  150.3 2.3 %broadcast_select_fusion.4 = bf16[32,384,128]{2,1,0:T(8,128)(2,1)S(1)} fusion(bf16[32,384,128]{2,1,0:T(8,128)(2,1)} %gather_fusion.9, pred[32]{0:T(512)(128)(4,1)S(1)} %copy-done.5), kind=kLoop, calls=%fused_computation.18 | loop fusion | flops 1572864 | bytes 6291488 | tf_op jit(solution)/shard_map/jit(_take)/select_n | solution.py:71
  152.6 6.4 %fusion = f32[4,384,128,1]{2,1,3,0:T(8,128)S(1)} fusion(bf16[4,8,384,128]{3,2,1,0:T(8,128)(2,1)S(1)} %bitcast.55, bf16[4,8,384,384]{3,2,1,0:T(8,128)(2,1)} %bitcast.44, pred[4,8]{1,0:T(4,128)(4,1)S(1)} %copy-done.11), kind=kOutput, calls=%fused_computation.12 | convolution fusion | flops 1212678144 | bytes 13369376 | tf_op jit(solution)/shard_map/rkij,rkjn->rin/dot_general | solution.py:74
  159.0 1.5 dynamic-slice_add_fusion
  (62 shorter events, 5.4 us)
Async XLA Ops:
  6.5 76.0 %copy-start.8 = (s32[4,8]{1,0:T(4,128)S(1)}, s32[4,8]{1,0:T(4,128)}, u32[]{:S(2)}) copy-start(s32[4,8]{1,0:T(4,128)} %param.12) | copy-start | bytes 388
  6.5 76.1 %copy-start.9 = (s32[1,32]{1,0:T(1,128)S(1)}, s32[1,32]{1,0:T(1,128)}, u32[]{:S(2)}) copy-start(s32[1,32]{1,0:T(1,128)} %param.11) | copy-start | bytes 388
  6.5 89.4 %all-gather.2.cloned.1.call-start = ((), (), s32[]{:S(2)}) async-start(), calls=%async_computation | async-start | bytes 10027008 | tf_op jit(solution)/shard_map/all_gather | solution.py:54
  45.7 68.5 %copy-start.2 = (s32[1024]{0:T(1024)}, s32[1024]{0:T(1024)S(1)}, u32[]{:S(2)}) copy-start(s32[1024]{0:T(1024)S(1)} %pad_clamp_fusion.2) | copy-start | bytes 12292
  67.7 47.1 %copy-start.6 = (pred[2]{0:T(512)(128)(4,1)}, pred[2]{0:T(512)(128)(4,1)S(1)}, u32[]{:S(2)}) copy-start(pred[2]{0:T(512)(128)(4,1)S(1)} %compare_and_fusion.2) | copy-start | bytes 10
  67.8 16.6 %collective-permute-start = (bf16[2,384,128]{2,1,0:T(8,128)(2,1)S(1)}, bf16[2,384,128]{2,1,0:T(8,128)(2,1)S(1)}, u32[]{:S(2)}, u32[]{:S(2)}) collective-permute-start(bf16[2,384,128]{2,1,0:T(8,128)(2,1)S(1)} %broadcast_select_fusion.12), channel_id=1, source_target_pairs={{0,16},{16,32},{32,48},{48,64},{64,80},{80,96},{96,112},{112,128},... | collective-permute-start | bytes 589832 | tf_op jit(solution)/shard_map/ppermute | solution.py:13
  81.8 31.8 %copy-start.3 = (s32[1024]{0:T(1024)}, s32[1024]{0:T(1024)S(1)}, u32[]{:S(2)}) copy-start(s32[1024]{0:T(1024)S(1)} %pad_clamp_fusion.1) | copy-start | bytes 12292
  82.4 32.3 %copy-start.7 = (pred[2]{0:T(512)(128)(4,1)}, pred[2]{0:T(512)(128)(4,1)S(1)}, u32[]{:S(2)}) copy-start(pred[2]{0:T(512)(128)(4,1)S(1)} %compare_and_fusion.1) | copy-start | bytes 10
  82.5 6.7 %collective-permute-start.1 = (bf16[2,384,128]{2,1,0:T(8,128)(2,1)S(1)}, bf16[2,384,128]{2,1,0:T(8,128)(2,1)S(1)}, u32[]{:S(2)}, u32[]{:S(2)}) collective-permute-start(bf16[2,384,128]{2,1,0:T(8,128)(2,1)S(1)} %broadcast_select_fusion.9), channel_id=1, source_target_pairs={{0,240},{16,0},{32,16},{48,32},{64,48},{80,64},{96,80},{112,96},{1... | collective-permute-start | bytes 589832 | tf_op jit(solution)/shard_map/ppermute | solution.py:13
  83.4 46.0 %copy-start.10 = (pred[4,8]{1,0:T(4,128)(4,1)}, pred[4,8]{1,0:T(4,128)(4,1)S(1)}, u32[]{:S(2)}) copy-start(pred[4,8]{1,0:T(4,128)(4,1)S(1)} %broadcast_in_dim.40) | copy-start | bytes 100
  83.4 41.1 %copy-start.1 = (s32[1024]{0:T(1024)}, s32[1024]{0:T(1024)S(1)}, u32[]{:S(2)}) copy-start(s32[1024]{0:T(1024)S(1)} %pad_clamp_fusion) | copy-start | bytes 12292
  83.5 43.7 %copy-start.4 = (pred[32]{0:T(512)(128)(4,1)}, pred[32]{0:T(512)(128)(4,1)S(1)}, u32[]{:S(2)}) copy-start(pred[32]{0:T(512)(128)(4,1)S(1)} %compare_and_fusion) | copy-start | bytes 100
  114.9 5.8 %collective-permute-start.2 = (bf16[2,384,128]{2,1,0:T(8,128)(2,1)S(1)}, bf16[2,384,128]{2,1,0:T(8,128)(2,1)S(1)}, u32[]{:S(2)}, u32[]{:S(2)}) collective-permute-start(bf16[2,384,128]{2,1,0:T(8,128)(2,1)S(1)} %broadcast_select_fusion.11), channel_id=1, source_target_pairs={{0,16},{16,32},{32,48},{48,64},{64,80},{80,96},{96,112},{112,128},... | collective-permute-start | bytes 589832 | tf_op jit(solution)/shard_map/ppermute | solution.py:13
  118.2 6.3 %collective-permute-start.3 = (bf16[2,384,128]{2,1,0:T(8,128)(2,1)S(1)}, bf16[2,384,128]{2,1,0:T(8,128)(2,1)S(1)}, u32[]{:S(2)}, u32[]{:S(2)}) collective-permute-start(bf16[2,384,128]{2,1,0:T(8,128)(2,1)S(1)} %broadcast_select_fusion.8), channel_id=1, source_target_pairs={{0,240},{16,0},{32,16},{48,32},{64,48},{80,64},{96,80},{112,96},{1... | collective-permute-start | bytes 589832 | tf_op jit(solution)/shard_map/ppermute | solution.py:13
  140.0 2.6 %collective-permute-start.4 = (bf16[2,384,128]{2,1,0:T(8,128)(2,1)S(1)}, bf16[2,384,128]{2,1,0:T(8,128)(2,1)S(1)}, u32[]{:S(2)}, u32[]{:S(2)}) collective-permute-start(bf16[2,384,128]{2,1,0:T(8,128)(2,1)S(1)} %broadcast_select_fusion.10), channel_id=1, source_target_pairs={{0,16},{16,32},{32,48},{48,64},{64,80},{80,96},{96,112},{112,128},... | collective-permute-start | bytes 589832 | tf_op jit(solution)/shard_map/ppermute | solution.py:13
  140.0 6.4 %collective-permute-start.5 = (bf16[2,384,128]{2,1,0:T(8,128)(2,1)S(1)}, bf16[2,384,128]{2,1,0:T(8,128)(2,1)}, u32[]{:S(2)}, u32[]{:S(2)}) collective-permute-start(bf16[2,384,128]{2,1,0:T(8,128)(2,1)S(1)} %broadcast_select_fusion.7), channel_id=1, source_target_pairs={{0,240},{16,0},{32,16},{48,32},{64,48},{80,64},{96,80},{112,96},{1... | collective-permute-start | bytes 589832 | tf_op jit(solution)/shard_map/ppermute | solution.py:13
  142.7 0.7 copy-start
  147.6 2.7 %copy-start.5 = (pred[32]{0:T(512)(128)(4,1)S(1)}, pred[32]{0:T(512)(128)(4,1)}, u32[]{:S(2)}) copy-start(pred[32]{0:T(512)(128)(4,1)} %copy-done.4) | copy-start | bytes 100
  150.3 2.3 %copy-start.11 = (pred[4,8]{1,0:T(4,128)(4,1)S(1)}, pred[4,8]{1,0:T(4,128)(4,1)}, u32[]{:S(2)}) copy-start(pred[4,8]{1,0:T(4,128)(4,1)} %copy-done.10) | copy-start | bytes 100
Sparse Core Ops, SparseCore 0:
  9.8 86.1 all-gather.1
where the time goes:
time: 168 us; the launch traced here: 167 us
  blocking collectives  55.8 us (33%)
  local copies, waits for them, and re-layouts  26.2 us (16%)
  matrix products  20.1 us (12%)
  waiting for transfers between devices  18 us (11%)
  starting transfers between devices  17.7 us (11%)
  other arithmetic  15.2 us (9%)
  between operations  14.4 us (9%)
    unnamed x1, blocking collectives  34.7 us
    all_gather x1, blocking collectives, local(): lax.all_gather(residual, 'grp', axis=0, tiled=True)  21.1 us
    dot_general x3, matrix products, apply_operator(): jnp.einsum('rkij,rkjn->rin', ordered, operand, preferred_element_type=jnp...  20.1 us
    ppermute x6, starting transfers between devices, from_behind(): lax.ppermute(shard, axis, [(i, (i + by) % devices) for i in range(devices)])  17.7 us
    ppermute x6, waiting for transfers between devices, from_behind(): lax.ppermute(shard, axis, [(i, (i + by) % devices) for i in range(devices)])  17.2 us
    gather x1, local copies, waits for them, and re-layouts, local(): ordered = jnp.take(group_tiles, placed, axis=0)  9.76 us
    select_n x4, other arithmetic, apply_operator(): jnp.take(extended, flat_cols, axis=0)  8.43 us
    gather x3, local copies, waits for them, and re-layouts, apply_operator(): jnp.take(extended, flat_cols, axis=0)  7.96 us
  transfers between devices with their start and end apart: 7, of which 7 were waited for; matrix products, arithmetic and copies ran while one was open for 7% of the time, Pallas kernels for 0%

commit v1 on v0

--- a/solution.py
+++ b/solution.py
@@ -52,8 +52,20 @@
     share_rows = residual.shape[0]
     group_slots = tile_slot[0]
     group_tiles = lax.all_gather(matrix_tiles, "grp", axis=0, tiled=True)
+
+    def _follow_widths(my_tile, dim_at):
+        return jnp.concatenate(
+            lax.all_to_all(
+                jnp.stack(lax.psum(1, axis_name="grp") * [my_tile], axis=0),
+                axis_name="grp",
+                split_axis=0,
+                concat_axis=0,
+            ),
+            dim_at,
+        )
+
     full_residual, full_inverse = (
-        lax.all_gather(residual, "grp", axis=0, tiled=True),
+        _follow_widths(residual, 0),
         lax.all_gather(diag_inv, "grp", axis=0, tiled=True),
     )
     placed = (

time: 168 us -> 162 us (0.964)
  blocking collectives: 55.8 us -> 34.4 us
  waiting for transfers between devices: 18 us -> 26.4 us
  starting transfers between devices: 17.7 us -> 21.8 us
  local copies, waits for them, and re-layouts: 26.2 us -> 28.2 us
    all_gather x1 -> x0, blocking collectives: 21.1 us -> none  [local(): lax.all_gather(residual, 'grp', axis=0, tiled=True)]
    all_gather x1, waiting for transfers between devices: 0.12 us -> 10 us  [local(): group_tiles = lax.all_gather(matrix_tiles, 'grp', axis=0, tiled=True)]
    all_to_all x0 -> x1, starting transfers between devices: none -> 6.75 us  [_follow_widths(): lax.all_to_all(jnp.stack(lax.psum(1, axis_name='grp') * [my_tile], axis=0...]
    mul x0 -> x1, other arithmetic: none -> 2.81 us  [one_sweep(): update = inverse[:, None] * start_residual / center_value]
    ppermute x6, starting transfers between devices: 17.7 us -> 15.1 us  [from_behind(): lax.ppermute(shard, axis, [(i, (i + by) % devices) for i in range(devices)])]
    another operation x0 -> x1, local copies, waits for them, and re-layouts: none -> 1.76 us  [_follow_widths(): jnp.stack(lax.psum(1, axis_name='grp') * [my_tile], axis=0)]
  transfers between devices with their start and end apart: 7 -> 8, of which waited for: 7 -> 6; matrix products, arithmetic and copies ran while one was open for 7% -> 11% of each run, Pallas kernels for 0% -> 0%
where the time goes in v1:
time: 162 us; the launch traced here: 161 us
  blocking collectives  34.4 us (21%)
  local copies, waits for them, and re-layouts  28.2 us (17%)
  waiting for transfers between devices  26.4 us (16%)
  starting transfers between devices  21.8 us (13%)
  matrix products  20 us (12%)
  other arithmetic  15.8 us (10%)
  between operations  14.4 us (9%)
    unnamed x1, blocking collectives  34.4 us
    dot_general x3, matrix products, apply_operator(): jnp.einsum('rkij,rkjn->rin', ordered, operand, preferred_element_type=jnp...  20 us
    ppermute x6, waiting for transfers between devices, from_behind(): lax.ppermute(shard, axis, [(i, (i + by) % devices) for i in range(devices)])  15.6 us
    ppermute x6, starting transfers between devices, from_behind(): lax.ppermute(shard, axis, [(i, (i + by) % devices) for i in range(devices)])  15.1 us
    all_gather x1, waiting for transfers between devices, local(): group_tiles = lax.all_gather(matrix_tiles, 'grp', axis=0, tiled=True)  10 us
    gather x1, local copies, waits for them, and re-layouts, local(): ordered = jnp.take(group_tiles, placed, axis=0)  9.56 us
    select_n x4, other arithmetic, apply_operator(): jnp.take(extended, flat_cols, axis=0)  8.43 us
    gather x3, local copies, waits for them, and re-layouts, apply_operator(): jnp.take(extended, flat_cols, axis=0)  7.79 us
  transfers between devices with their start and end apart: 8, of which 6 were waited for; matrix products, arithmetic and copies ran while one was open for 11% of the time, Pallas kernels for 0%

profile of v1, /device:TPU:97, one launch (start us, length us, event | category | flops | bytes accessed | tf_op | source)
XLA Modules:
  0.0 160.9 jit_solution(15094535875497609346)
XLA Ops:
  6.5 0.7 all-gather.2.cloned.1.call-update
  7.3 1.8 %stack.2 = f32[16,96,128]{2,1,0:T(8,128)} broadcast(f32[96,128]{1,0:T(8,128)} %param.14), dimensions={1,2} | broadcast | bytes 835584 | tf_op jit(solution)/shard_map/stack | solution.py:59
  9.0 6.8 %all-to-all-start = ((f32[16,96,128]{2,1,0:T(8,128)}), f32[16,96,128]{2,1,0:T(8,128)S(1)}, u32[]{:S(2)}, u32[]{:S(2)}) async-start(f32[16,96,128]{2,1,0:T(8,128)} %stack.2), calls=%async_computation | async-start | bytes 1572864 | tf_op jit(solution)/shard_map/all_to_all | solution.py:58
  15.8 0.8 reshape.122
  16.6 0.7 fusion.28
  17.2 0.7 scatter_custom_fusion
  18.0 1.3 dynamic-slice
  19.9 0.9 dynamic-update-slice
  20.8 34.4 %all-reduce = f32[1536]{0:T(1024)S(1)} all-reduce(f32[1536]{0:T(1024)S(1)} %dynamic-update-slice), channel_id=1, replica_groups=mesh['lead'=16,'grp'=16] {'grp'}, use_global_device_ids=true, to_apply=%add | all-reduce | flops 1536 | bytes 12288
  55.2 0.9 fusion.26
  57.8 11.3 %collective-permute-start = (bf16[2,384,128]{2,1,0:T(8,128)(2,1)S(1)}, bf16[2,384,128]{2,1,0:T(8,128)(2,1)S(1)}, u32[]{:S(2)}, u32[]{:S(2)}) collective-permute-start(bf16[2,384,128]{2,1,0:T(8,128)(2,1)S(1)} %broadcast_select_fusion.12), channel_id=1, source_target_pairs={{0,16},{16,32},{32,48},{48,64},{64,80},{80,96},{96,112},{112,128},... | collective-permute-start | bytes 589832 | tf_op jit(solution)/shard_map/ppermute | solution.py:13
  69.2 2.5 %collective-permute-done = bf16[2,384,128]{2,1,0:T(8,128)(2,1)S(1)} collective-permute-done((bf16[2,384,128]{2,1,0:T(8,128)(2,1)S(1)}, bf16[2,384,128]{2,1,0:T(8,128)(2,1)S(1)}, u32[]{:S(2)}, u32[]{:S(2)}) %collective-permute-start) | collective-permute-done | bytes 196640 | tf_op jit(solution)/shard_map/ppermute | solution.py:13
  71.7 4.2 %collective-permute-done.1 = bf16[2,384,128]{2,1,0:T(8,128)(2,1)S(1)} collective-permute-done((bf16[2,384,128]{2,1,0:T(8,128)(2,1)S(1)}, bf16[2,384,128]{2,1,0:T(8,128)(2,1)S(1)}, u32[]{:S(2)}, u32[]{:S(2)}) %collective-permute-start.1) | collective-permute-done | bytes 196640 | tf_op jit(solution)/shard_map/ppermute | solution.py:13
  76.0 2.6 %gather_fusion.3 = bf16[32,384,128]{2,1,0:T(8,128)(2,1)} fusion(bf16[8,384,128]{2,1,0:T(8,128)(2,1)S(1)} %pad_maximum_fusion, s32[1024]{0:T(1024)S(1)} %pad_clamp_fusion), kind=kCustom, calls=%fused_computation.1.clone | custom fusion | bytes 6291584 | tf_op jit(solution)/shard_map/jit(_take)/gather | solution.py:83
  78.6 3.9 %broadcast_select_fusion.6 = bf16[32,384,128]{2,1,0:T(8,128)(2,1)} fusion(bf16[32,384,128]{2,1,0:T(8,128)(2,1)} %gather_fusion.3, pred[32]{0:T(512)(128)(4,1)S(1)} %compare_and_fusion), kind=kLoop, calls=%fused_computation.20 | loop fusion | flops 1572864 | bytes 6291488 | tf_op jit(solution)/shard_map/jit(_take)/select_n | solution.py:83
  82.6 10.0 %all-gather.2.cloned.1.call-done = bf16[32,384,384]{2,1,0:T(8,128)(2,1)} async-done(((bf16[2,384,384]{2,1,0:T(8,128)(2,1)}), bf16[32,384,384]{2,1,0:T(8,128)(2,1)}) %all-gather.2.cloned.1.call-update) | async-done | bytes 9437200 | tf_op jit(solution)/shard_map/all_gather | solution.py:54
  92.6 9.6 %gather_fusion = bf16[32,384,384]{2,1,0:T(8,128)(2,1)} fusion(bf16[32,384,384]{2,1,0:T(8,128)(2,1)} %all-gather.2.cloned.1.call-done, s32[1024]{0:T(1024)S(1)} %pad_clamp_fusion.3), kind=kCustom, calls=%fused_computation.9 | custom fusion | bytes 18874496 | tf_op jit(solution)/shard_map/jit(_take)/gather | solution.py:76
  102.1 7.3 %fusion.2 = f32[4,384,128,1]{2,1,3,0:T(8,128)S(1)} fusion(bf16[4,8,384,128]{3,2,1,0:T(8,128)(2,1)} %bitcast.104, bf16[4,8,384,384]{3,2,1,0:T(8,128)(2,1)} %bitcast.101, pred[4,8]{1,0:T(4,128)(4,1)S(1)} %broadcast_in_dim.40), kind=kOutput, calls=%fused_computation.14 | convolution fusion | flops 1212678144 | bytes 13369376 | tf_op jit(solution)/shard_map/rkij,rkjn->rin/dot_general | solution.py:86
  111.3 3.2 %collective-permute-start.2 = (bf16[2,384,128]{2,1,0:T(8,128)(2,1)S(1)}, bf16[2,384,128]{2,1,0:T(8,128)(2,1)S(1)}, u32[]{:S(2)}, u32[]{:S(2)}) collective-permute-start(bf16[2,384,128]{2,1,0:T(8,128)(2,1)S(1)} %broadcast_select_fusion.11), channel_id=1, source_target_pairs={{0,16},{16,32},{32,48},{48,64},{64,80},{80,96},{96,112},{112,128},... | collective-permute-start | bytes 589832 | tf_op jit(solution)/shard_map/ppermute | solution.py:13
  114.6 2.5 %collective-permute-done.2 = bf16[2,384,128]{2,1,0:T(8,128)(2,1)S(1)} collective-permute-done((bf16[2,384,128]{2,1,0:T(8,128)(2,1)S(1)}, bf16[2,384,128]{2,1,0:T(8,128)(2,1)S(1)}, u32[]{:S(2)}, u32[]{:S(2)}) %collective-permute-start.2) | collective-permute-done | bytes 196640 | tf_op jit(solution)/shard_map/ppermute | solution.py:13
  117.1 3.7 %collective-permute-done.3 = bf16[2,384,128]{2,1,0:T(8,128)(2,1)S(1)} collective-permute-done((bf16[2,384,128]{2,1,0:T(8,128)(2,1)S(1)}, bf16[2,384,128]{2,1,0:T(8,128)(2,1)S(1)}, u32[]{:S(2)}, u32[]{:S(2)}) %collective-permute-start.3) | collective-permute-done | bytes 196640 | tf_op jit(solution)/shard_map/ppermute | solution.py:13
  120.9 2.6 %gather_fusion.6 = bf16[32,384,128]{2,1,0:T(8,128)(2,1)} fusion(bf16[8,384,128]{2,1,0:T(8,128)(2,1)S(1)} %pad_maximum_fusion.1, s32[1024]{0:T(1024)S(1)} %pad_clamp_fusion), kind=kCustom, calls=%fused_computation.7.clone | custom fusion | bytes 6291584 | tf_op jit(solution)/shard_map/jit(_take)/gather | solution.py:83
  123.5 2.2 %broadcast_select_fusion.5 = bf16[32,384,128]{2,1,0:T(8,128)(2,1)S(1)} fusion(bf16[32,384,128]{2,1,0:T(8,128)(2,1)} %gather_fusion.6, pred[32]{0:T(512)(128)(4,1)S(1)} %compare_and_fusion), kind=kLoop, calls=%fused_computation.19 | loop fusion | flops 1572864 | bytes 6291488 | tf_op jit(solution)/shard_map/jit(_take)/select_n | solution.py:83
  125.7 6.4 %fusion.1 = f32[4,384,128,1]{2,1,3,0:T(8,128)S(1)} fusion(bf16[4,8,384,128]{3,2,1,0:T(8,128)(2,1)S(1)} %bitcast.106, bf16[4,8,384,384]{3,2,1,0:T(8,128)(2,1)} %bitcast.102, pred[4,8]{1,0:T(4,128)(4,1)S(1)} %broadcast_in_dim.40), kind=kOutput, calls=%fused_computation.13 | convolution fusion | flops 1212678144 | bytes 13369376 | tf_op jit(solution)/shard_map/rkij,rkjn->rin/dot_general | solution.py:86
  132.1 0.9 copy-done
  133.5 0.6 gather_fusion.8
  135.4 2.8 %broadcast_multiply_fusion = (f32[1536,128]{1,0:T(8,128)}, f32[1536,128]{1,0:T(8,128)S(1)}, f32[1536,128]{1,0:T(8,128)}) fusion(f32[1536]{0:T(1024)S(1)} %all-reduce, f32[4,384,128,1]{2,1,3,0:T(8,128)} %copy-done, f32[16,96,128]{2,1,0:T(8,128)S(1)} %all-to-all-done, f32[4,384,128,1]{2,1,3,0:T(8,128)S(1)} %fusion.2, f32[1536]{0:T(1024)S(1)} %broadcast_multiply_fusion.1), kind=kLoop, calls=%fused_computation.47 | loop fusion | flops 2359296 | bytes 4730880 | tf_op jit(solution)/shard_map/mul | solution.py:20
  138.5 2.7 %collective-permute-done.5 = bf16[2,384,128]{2,1,0:T(8,128)(2,1)S(1)} collective-permute-done((bf16[2,384,128]{2,1,0:T(8,128)(2,1)S(1)}, bf16[2,384,128]{2,1,0:T(8,128)(2,1)S(1)}, u32[]{:S(2)}, u32[]{:S(2)}) %collective-permute-start.5) | collective-permute-done | bytes 196640 | tf_op jit(solution)/shard_map/ppermute | solution.py:13
  141.3 2.6 %gather_fusion.9 = bf16[32,384,128]{2,1,0:T(8,128)(2,1)} fusion(bf16[8,384,128]{2,1,0:T(8,128)(2,1)S(1)} %pad_maximum_fusion.2, s32[1024]{0:T(1024)S(1)} %pad_clamp_fusion), kind=kCustom, calls=%fused_computation.8.clone | custom fusion | bytes 6291584 | tf_op jit(solution)/shard_map/jit(_take)/gather | solution.py:83
  143.9 2.2 %broadcast_select_fusion.4 = bf16[32,384,128]{2,1,0:T(8,128)(2,1)S(1)} fusion(bf16[32,384,128]{2,1,0:T(8,128)(2,1)} %gather_fusion.9, pred[32]{0:T(512)(128)(4,1)S(1)} %compare_and_fusion), kind=kLoop, calls=%fused_computation.18 | loop fusion | flops 1572864 | bytes 6291488 | tf_op jit(solution)/shard_map/jit(_take)/select_n | solution.py:83
  146.2 6.4 %fusion = f32[4,384,128,1]{2,1,3,0:T(8,128)S(1)} fusion(bf16[4,8,384,128]{3,2,1,0:T(8,128)(2,1)S(1)} %bitcast.105, bf16[4,8,384,384]{3,2,1,0:T(8,128)(2,1)} %bitcast.103, pred[4,8]{1,0:T(4,128)(4,1)S(1)} %broadcast_in_dim.40), kind=kOutput, calls=%fused_computation.12 | convolution fusion | flops 1212678144 | bytes 13369376 | tf_op jit(solution)/shard_map/rkij,rkjn->rin/dot_general | solution.py:86
  152.5 1.5 dynamic-slice_add_fusion
  (45 shorter events, 6.0 us)
Async XLA Ops:
  6.5 86.0 %all-gather.2.cloned.1.call-start = ((), (), s32[]{:S(2)}) async-start(), calls=%async_computation.1 | async-start | bytes 10027008 | tf_op jit(solution)/shard_map/all_gather | solution.py:54
  9.0 47.2 %all-to-all-start = ((f32[16,96,128]{2,1,0:T(8,128)}), f32[16,96,128]{2,1,0:T(8,128)S(1)}, u32[]{:S(2)}, u32[]{:S(2)}) async-start(f32[16,96,128]{2,1,0:T(8,128)} %stack.2), calls=%async_computation | async-start | bytes 1572864 | tf_op jit(solution)/shard_map/all_to_all | solution.py:58
  57.8 13.9 %collective-permute-start = (bf16[2,384,128]{2,1,0:T(8,128)(2,1)S(1)}, bf16[2,384,128]{2,1,0:T(8,128)(2,1)S(1)}, u32[]{:S(2)}, u32[]{:S(2)}) collective-permute-start(bf16[2,384,128]{2,1,0:T(8,128)(2,1)S(1)} %broadcast_select_fusion.12), channel_id=1, source_target_pairs={{0,16},{16,32},{32,48},{48,64},{64,80},{80,96},{96,112},{112,128},... | collective-permute-start | bytes 589832 | tf_op jit(solution)/shard_map/ppermute | solution.py:13
  69.2 6.7 %collective-permute-start.1 = (bf16[2,384,128]{2,1,0:T(8,128)(2,1)S(1)}, bf16[2,384,128]{2,1,0:T(8,128)(2,1)S(1)}, u32[]{:S(2)}, u32[]{:S(2)}) collective-permute-start(bf16[2,384,128]{2,1,0:T(8,128)(2,1)S(1)} %broadcast_select_fusion.9), channel_id=1, source_target_pairs={{0,240},{16,0},{32,16},{48,32},{64,48},{80,64},{96,80},{112,96},{1... | collective-permute-start | bytes 589832 | tf_op jit(solution)/shard_map/ppermute | solution.py:13
  111.3 5.8 %collective-permute-start.2 = (bf16[2,384,128]{2,1,0:T(8,128)(2,1)S(1)}, bf16[2,384,128]{2,1,0:T(8,128)(2,1)S(1)}, u32[]{:S(2)}, u32[]{:S(2)}) collective-permute-start(bf16[2,384,128]{2,1,0:T(8,128)(2,1)S(1)} %broadcast_select_fusion.11), channel_id=1, source_target_pairs={{0,16},{16,32},{32,48},{48,64},{64,80},{80,96},{96,112},{112,128},... | collective-permute-start | bytes 589832 | tf_op jit(solution)/shard_map/ppermute | solution.py:13
  114.5 6.3 %collective-permute-start.3 = (bf16[2,384,128]{2,1,0:T(8,128)(2,1)S(1)}, bf16[2,384,128]{2,1,0:T(8,128)(2,1)S(1)}, u32[]{:S(2)}, u32[]{:S(2)}) collective-permute-start(bf16[2,384,128]{2,1,0:T(8,128)(2,1)S(1)} %broadcast_select_fusion.8), channel_id=1, source_target_pairs={{0,240},{16,0},{32,16},{48,32},{64,48},{80,64},{96,80},{112,96},{1... | collective-permute-start | bytes 589832 | tf_op jit(solution)/shard_map/ppermute | solution.py:13
  132.1 0.9 copy-start
  134.9 3.6 %collective-permute-start.4 = (bf16[2,384,128]{2,1,0:T(8,128)(2,1)S(1)}, bf16[2,384,128]{2,1,0:T(8,128)(2,1)S(1)}, u32[]{:S(2)}, u32[]{:S(2)}) collective-permute-start(bf16[2,384,128]{2,1,0:T(8,128)(2,1)S(1)} %broadcast_select_fusion.10), channel_id=1, source_target_pairs={{0,16},{16,32},{32,48},{48,64},{64,80},{80,96},{96,112},{112,128},... | collective-permute-start | bytes 589832 | tf_op jit(solution)/shard_map/ppermute | solution.py:13
  134.9 6.3 %collective-permute-start.5 = (bf16[2,384,128]{2,1,0:T(8,128)(2,1)S(1)}, bf16[2,384,128]{2,1,0:T(8,128)(2,1)S(1)}, u32[]{:S(2)}, u32[]{:S(2)}) collective-permute-start(bf16[2,384,128]{2,1,0:T(8,128)(2,1)S(1)} %broadcast_select_fusion.7), channel_id=1, source_target_pairs={{0,240},{16,0},{32,16},{48,32},{64,48},{80,64},{96,80},{112,96},{1... | collective-permute-start | bytes 589832 | tf_op jit(solution)/shard_map/ppermute | solution.py:13
Sparse Core Ops, SparseCore 0:
  9.8 82.7 all-gather.1
